TPU v7x, 32 devices: a whole 2x2x4 slice. The times are simulated.
32 devices in a mesh: cuts: 2 (over x), mode: 8 (over z, y), branch: 2 (over core).
Axes of the slice: x: 2, y: 2, z: 4, core: 2. Of those that a mesh axis runs over, the one named last changes fastest.
Arguments:
- leaves: bfloat16 [8, 2, 32, 512, 512], P('branch', None, ('cuts', 'mode')), parts along dimension 2, may hold values from -0.1875 to 0.1875
- join_order: int32 [7], replicated, may hold values from 0 to 1
- slice_values: int32 [32], P(('cuts', 'mode')), parts along dimension 0, may hold values from 0 to 1
- boundary: bfloat16 [2, 2, 512, 512], replicated, may hold values from -4 to 4
Outputs:
- amplitudes: float32 [2, 32, 512, 512], P(None, ('cuts', 'mode'), 'branch'), parts along dimension 1
There are 2 independent parts, one for each index of `cuts`. A program takes and returns all parts, laid end to end along the dimension named above; an argument that names none is the same for every part. Nothing has to cross between parts.
Inputs may be any that keep to these rules, and one draw needn't show every extreme that they name: `join_order`: 1 puts the second operand of the join on the left.
All inputs are finite; a program needn't handle non-finite values.
Results may differ from a plain program's by a relative error of at most 0.0076.
Values may be sent and summed in bfloat16 or wider, within the bound.
A program may use at most 64 MiB of HBM per device.

v0:
```python
import jax
import jax.numpy as jnp
from jax import lax
from jax.sharding import PartitionSpec as P


def from_partner(value, axis, bit):
    mask = 2**bit
    pairs = [(source, source ^ mask) for source in range(lax.axis_size(axis))]
    return lax.ppermute(value, axis, pairs)


def complex_sums(left_op, right_op):
    spec = "bij,bjk->bik"
    real_part = jnp.einsum(
        spec, left_op[0], right_op[0], preferred_element_type=jnp.float32
    ) - jnp.einsum(spec, left_op[1], right_op[1], preferred_element_type=jnp.float32)
    imag_part = jnp.einsum(
        spec, left_op[0], right_op[1], preferred_element_type=jnp.float32
    ) + jnp.einsum(spec, left_op[1], right_op[0], preferred_element_type=jnp.float32)
    return jnp.stack([real_part, imag_part])


def complex_product(left_op, right_op):
    return complex_sums(left_op, right_op).astype(jnp.bfloat16)


def join_pair(left_op, right_op, swapped):
    return lax.cond(
        swapped == 1,
        lambda: complex_product(right_op, left_op),
        lambda: complex_product(left_op, right_op),
    )


def split_rows(tensor, blocks):
    shape = tensor.shape
    return tensor.reshape(shape[0], shape[1], blocks, shape[2] // blocks, shape[3])


def merge_rows(tensor):
    shape = tensor.shape
    width = shape[4]
    total_rows = shape[1] * shape[2] * shape[3]
    return tensor.reshape(shape[0], total_rows // width, width, width)


def per_device(leaves, join_order, slice_values, boundary):
    blocks = lax.axis_size("mode")
    branch_index = lax.axis_index("branch")
    base_index = 2 * branch_index
    first_pair = join_pair(leaves[0], leaves[1], join_order[base_index])
    second_pair = join_pair(leaves[2], leaves[3], join_order[base_index + 1])
    first_pair, second_pair = (
        lax.all_to_all(
            split_rows(first_pair, blocks), "mode", split_axis=2, concat_axis=1, tiled=True
        ),
        lax.all_to_all(
            split_rows(second_pair, blocks), "mode", split_axis=2, concat_axis=1, tiled=True
        ),
    )
    first_pair = merge_rows(first_pair)
    second_pair = merge_rows(second_pair)
    middle = join_pair(first_pair, second_pair, join_order[4 + branch_index])
    middle = merge_rows(
        lax.all_to_all(split_rows(middle, blocks), "mode", split_axis=2, concat_axis=1, tiled=True)
    )
    width = middle.shape[3]
    half_rows = width // 2
    chosen = jnp.where(
        slice_values[None, :, None, None] == 1, boundary[1][:, None], boundary[0][:, None]
    )
    top_order = join_order[-1]
    partner = from_partner(middle, "branch", 0)
    is_first = branch_index == 0
    upper = jnp.where(is_first, middle, partner)
    lower = jnp.where(is_first, partner, middle)
    leading = jnp.where(top_order == 1, lower, upper)
    trailing = jnp.where(top_order == 1, upper, lower)
    leading = lax.dynamic_slice_in_dim(leading, branch_index * half_rows, half_rows, 2)
    top_half = complex_product(leading, trailing)
    amplitudes = complex_sums(top_half, chosen)
    return amplitudes


def solution(mesh):
    in_specs = (P("branch", None, ("cuts", "mode"), None, None), P(), P(("cuts", "mode")), P())
    out_specs = P(None, ("cuts", "mode"), "branch", None)
    return jax.shard_map(
        per_device, mesh=mesh, in_specs=in_specs, out_specs=out_specs, check_vma=False
    )
```

profile of v0, /device:TPU:0, one launch (start us, length us, event | category | flops | bytes accessed | tf_op | source)
XLA Modules:
  0.0 195.7 jit_solution(156778789101351986)
XLA Ops:
  0.0 5.7 %slice_bitcast_fusion = (bf16[2,2,512,512]{3,2,1,0:T(8,128)(2,1)}, bf16[2,2,512,512]{3,2,1,0:T(8,128)(2,1)S(1)}, bf16[2,2,512,512]{3,2,1,0:T(8,128)(2,1)}, bf16[2,2,512,512]{3,2,1,0:T(8,128)(2,1)}) fusion(bf16[4,2,2,512,512]{4,3,2,1,0:T(8,128)(2,1)} %param.10), kind=kLoop, calls=%fused_computation.127 | loop fusion | bytes 16777216 | tf_op jit(solution)/shard_map/squeeze | solution.py:53
  5.7 0.7 fusion.116
  7.0 6.6 %conditional.7 = (bf16[2,2,512,512]{3,2,1,0:T(8,128)(2,1)}) conditional(s32[]{:T(128)} %bitcast.45, (bf16[2,2,512,512]{3,2,1,0:T(8,128)(2,1)}, bf16[2,2,512,512]{3,2,1,0:T(8,128)(2,1)}) %tuple.34, (bf16[2,2,512,512]{3,2,1,0:T(8,128)(2,1)}, bf16[2,2,512,512]{3,2,1,0:T(8,128)(2,1)}) %tuple.35), branch_computations={%region_2.0_spmd, %region_3.0_spmd} | conditional | flops 2150629376 | bytes 39845952
  7.0 0.0 copy-start.2
  7.1 2.4 %fusion.36 = f32[2,512,512]{2,1,0:T(8,128)S(1)} fusion(bf16[2,2,512,512]{3,2,1,0:T(8,128)(2,1)} %get-tuple-element.49, bf16[2,2,512,512]{3,2,1,0:T(8,128)(2,1)} %get-tuple-element.48), kind=kOutput, calls=%fused_computation.45 | convolution fusion | flops 536870912 | bytes 4194304 | tf_op jit(solution)/shard_map/cond/branch_0_fun/bij,bjk->bik/dot_general | solution.py:18
  9.5 0.4 copy-done.4
  9.9 0.7 add_bitcast_fusion.2
  10.6 0.7 fusion.42
  11.3 0.7 subtract_bitcast_fusion.2
  12.1 1.6 pad_maximum_fusion.2
  13.6 3.2 %copy.11 = bf16[2,2,8,64,512]{4,3,1,0,2:T(8,128)(2,1)} copy(bf16[2,2,8,64,512]{4,3,2,1,0:T(8,128)(2,1)} %bitcast.213) | data formatting | bytes 4194304 | tf_op jit(solution)/shard_map/reshape | solution.py:38
  16.8 7.3 %all-to-all-start.1 = ((bf16[2,2,8,64,512]{4,3,1,0,2:T(8,128)(2,1)}), bf16[2,2,8,64,512]{4,3,1,0,2:T(8,128)(2,1)}, u32[]{:S(2)}, u32[]{:S(2)}) async-start(bf16[2,2,8,64,512]{4,3,1,0,2:T(8,128)(2,1)} %copy.11), calls=%async_computation.1 | async-start | bytes 4194304 | tf_op jit(solution)/shard_map/all_to_all | solution.py:58
  24.7 4.5 %conditional.6 = (bf16[2,2,512,512]{3,2,1,0:T(8,128)(2,1)S(1)}) conditional(s32[]{:T(128)} %bitcast.38, (bf16[2,2,512,512]{3,2,1,0:T(8,128)(2,1)}, bf16[2,2,512,512]{3,2,1,0:T(8,128)(2,1)S(1)}) %tuple.32, (bf16[2,2,512,512]{3,2,1,0:T(8,128)(2,1)S(1)}, bf16[2,2,512,512]{3,2,1,0:T(8,128)(2,1)}) %tuple.33), branch_computations={%region_0.0_spmd, %region_1.0_spmd} | conditional | flops 2150629376 | bytes 31457316
  24.8 2.1 %fusion.18 = f32[2,512,512]{2,1,0:T(8,128)S(1)} fusion(bf16[2,2,512,512]{3,2,1,0:T(8,128)(2,1)} %get-tuple-element.47, bf16[2,2,512,512]{3,2,1,0:T(8,128)(2,1)S(1)} %get-tuple-element.46), kind=kOutput, calls=%fused_computation.24 | convolution fusion | flops 536870912 | bytes 4194304 | tf_op jit(solution)/shard_map/cond/branch_1_fun/bij,bjk->bik/dot_general | solution.py:18
  26.9 0.7 add_bitcast_fusion.1
  27.6 0.7 fusion.24
  28.3 0.7 subtract_bitcast_fusion.1
  29.0 0.2 pad_maximum_fusion.1
  29.2 1.5 copy.9
  30.7 41.7 %all-to-all-done.1 = bf16[2,2,8,64,512]{4,3,1,0,2:T(8,128)(2,1)} async-done(((bf16[2,2,8,64,512]{4,3,1,0,2:T(8,128)(2,1)}), bf16[2,2,8,64,512]{4,3,1,0,2:T(8,128)(2,1)}, u32[]{:S(2)}, u32[]{:S(2)}) %all-to-all-start.1) | async-done | bytes 2097184 | tf_op jit(solution)/shard_map/all_to_all | solution.py:58
  72.4 4.4 %all-to-all-start = ((bf16[2,2,8,64,512]{4,3,1,0,2:T(8,128)(2,1)}), bf16[2,2,8,64,512]{4,3,1,0,2:T(8,128)(2,1)}, u32[]{:S(2)}, u32[]{:S(2)}) async-start(bf16[2,2,8,64,512]{4,3,1,0,2:T(8,128)(2,1)} %copy.9), calls=%async_computation | async-start | bytes 4194304 | tf_op jit(solution)/shard_map/all_to_all | solution.py:55
  77.5 1.8 copy.12
  79.3 45.3 %all-to-all-done = bf16[2,2,8,64,512]{4,3,1,0,2:T(8,128)(2,1)} async-done(((bf16[2,2,8,64,512]{4,3,1,0,2:T(8,128)(2,1)}), bf16[2,2,8,64,512]{4,3,1,0,2:T(8,128)(2,1)}, u32[]{:S(2)}, u32[]{:S(2)}) %all-to-all-start) | async-done | bytes 2097184 | tf_op jit(solution)/shard_map/all_to_all | solution.py:55
  124.6 1.8 copy.10
  126.4 3.3 %conditional.8 = (bf16[2,2,512,512]{3,2,1,0:T(8,128)(2,1)S(1)}) conditional(s32[]{:T(128)} %bitcast.37, (bf16[2,2,512,512]{3,2,1,0:T(8,128)(2,1)S(1)}, bf16[2,2,512,512]{3,2,1,0:T(8,128)(2,1)S(1)}) %tuple.55, (bf16[2,2,512,512]{3,2,1,0:T(8,128)(2,1)S(1)}, bf16[2,2,512,512]{3,2,1,0:T(8,128)(2,1)S(1)}) %tuple.56), branch_computations={%region_4.0_spmd, %region_5.0_spmd} | conditional | flops 2150629376 | bytes 23068680
  126.4 0.7 fusion.72
  127.2 0.7 add_bitcast_fusion.4
  127.9 0.7 fusion.78
  128.6 0.7 subtract_bitcast_fusion.4
  129.3 0.2 pad_maximum_fusion.4
  129.7 0.2 copy.13
  129.9 51.8 %all_to_all.45 = bf16[2,2,8,64,512]{4,3,1,0,2:T(8,128)(2,1)S(1)} all-to-all(bf16[2,2,8,64,512]{4,3,1,0,2:T(8,128)(2,1)S(1)} %copy.13), channel_id=1, replica_groups=mesh['cuts'=2,'mode'=8,'branch'=2] {'mode'}, dimensions={2} | all-to-all | bytes 4194304 | tf_op jit(solution)/shard_map/all_to_all | solution.py:66
  181.7 1.5 copy.14
  183.3 0.0 collective-permute-start
  183.9 1.7 slice_bitcast_fusion.9
  185.6 0.3 broadcast_select_fusion
  185.9 1.9 collective-permute-done
  187.8 2.6 %broadcast_select_fusion.3 = (bf16[2,2,512,512]{3,2,1,0:T(8,128)(2,1)S(1)}, bf16[2,2,512,512]{3,2,1,0:T(8,128)(2,1)S(1)}, bf16[2,2,512,512]{3,2,1,0:T(8,128)(2,1)S(1)}) fusion(pred[]{:T(512)} %bitcast.36, bf16[2,2,512,512]{3,2,1,0:T(8,128)(2,1)} %collective-permute-done, bf16[2,2,512,512]{3,2,1,0:T(8,128)(2,1)} %bitcast.59, pred[]{:T(512)S(6)} %eq.28), kind=kLoop, calls=%fused_computation.134 | loop fusion | flops 3145728 | bytes 10485762 | tf_op jit(solution)/shard_map/jit(_where)/select_n | solution.py:79
  190.4 0.3 dynamic-slice_select_fusion
  190.7 0.4 fusion.113
  191.1 0.4 fusion.112
  191.6 0.4 fusion.110
  192.0 0.4 fusion.114
  192.5 0.4 fusion.115
  192.9 0.4 fusion.111
  193.4 0.4 fusion.109
  193.8 0.4 fusion.108
  194.2 1.5 pad_maximum_fusion.6
  (9 shorter events, 0.0 us)
Async XLA Ops:
  0.0 5.7 %copy-start.6 = (s32[7]{0:T(128)S(1)}, s32[7]{0:T(128)}, u32[]{:S(2)}) copy-start(s32[7]{0:T(128)} %param.11) | copy-start | bytes 88
  7.0 2.4 %copy-start.2 = (bf16[2,2,512,512]{3,2,1,0:T(8,128)(2,1)S(1)}, bf16[2,2,512,512]{3,2,1,0:T(8,128)(2,1)}, u32[]{:S(2)}) copy-start(bf16[2,2,512,512]{3,2,1,0:T(8,128)(2,1)} %get-tuple-element.49) | copy-start | bytes 6291460 | tf_op jit(solution)/shard_map/conditional.1
  7.1 2.8 %copy-start.4 = (bf16[2,2,512,512]{3,2,1,0:T(8,128)(2,1)S(1)}, bf16[2,2,512,512]{3,2,1,0:T(8,128)(2,1)}, u32[]{:S(2)}) copy-start(bf16[2,2,512,512]{3,2,1,0:T(8,128)(2,1)} %get-tuple-element.48) | copy-start | bytes 6291460 | tf_op jit(solution)/shard_map/conditional.1
  16.8 55.7 %all-to-all-start.1 = ((bf16[2,2,8,64,512]{4,3,1,0,2:T(8,128)(2,1)}), bf16[2,2,8,64,512]{4,3,1,0,2:T(8,128)(2,1)}, u32[]{:S(2)}, u32[]{:S(2)}) async-start(bf16[2,2,8,64,512]{4,3,1,0,2:T(8,128)(2,1)} %copy.11), calls=%async_computation.1 | async-start | bytes 4194304 | tf_op jit(solution)/shard_map/all_to_all | solution.py:58
  24.8 2.1 %copy-start.1 = (bf16[2,2,512,512]{3,2,1,0:T(8,128)(2,1)S(1)}, bf16[2,2,512,512]{3,2,1,0:T(8,128)(2,1)}, u32[]{:S(2)}) copy-start(bf16[2,2,512,512]{3,2,1,0:T(8,128)(2,1)} %get-tuple-element.47) | copy-start | bytes 6291460 | tf_op jit(solution)/shard_map/conditional
  72.4 52.2 %all-to-all-start = ((bf16[2,2,8,64,512]{4,3,1,0,2:T(8,128)(2,1)}), bf16[2,2,8,64,512]{4,3,1,0,2:T(8,128)(2,1)}, u32[]{:S(2)}, u32[]{:S(2)}) async-start(bf16[2,2,8,64,512]{4,3,1,0,2:T(8,128)(2,1)} %copy.9), calls=%async_computation | async-start | bytes 4194304 | tf_op jit(solution)/shard_map/all_to_all | solution.py:55
  181.7 2.2 %copy-start.7 = (s32[2]{0:T(128)S(1)}, s32[2]{0:T(128)}, u32[]{:S(2)}) copy-start(s32[2]{0:T(128)} %param.12) | copy-start | bytes 28
  183.3 4.5 %collective-permute-start = (bf16[2,2,512,512]{3,2,1,0:T(8,128)(2,1)}, bf16[2,2,512,512]{3,2,1,0:T(8,128)(2,1)}, u32[]{:S(2)}, u32[]{:S(2)}) collective-permute-start(bf16[2,2,512,512]{3,2,1,0:T(8,128)(2,1)} %bitcast.59), channel_id=1, source_target_pairs={{0,1},{1,0},{2,3},{3,2},{4,5},{5,4},{6,7},{7,6},{8,9},{9,8},{10,11... | collective-permute-start | bytes 6291464 | tf_op jit(solution)/shard_map/ppermute | solution.py:10
where the time goes:
time: 196 us
  waiting for transfers between devices  88.9 us (45%)
  blocking collectives  51.8 us (26%)
  local copies, waits for them, and re-layouts  18.6 us (9%)
  matrix products  15.1 us (8%)
  starting transfers between devices  11.7 us (6%)
  other arithmetic  6.63 us (3%)
  between operations  2.74 us (1%)
    all_to_all x1, blocking collectives, per_device(): lax.all_to_all(split_rows(middle, blocks), 'mode', split_axis=2, concat_a...  51.8 us
    all_to_all x1, waiting for transfers between devices, per_device(): lax.all_to_all(split_rows(first_pair, blocks), 'mode', split_axis=2, conc...  45.3 us
    all_to_all x1, waiting for transfers between devices, per_device(): lax.all_to_all(split_rows(second_pair, blocks), 'mode', split_axis=2, con...  41.7 us
    all_to_all x1, starting transfers between devices, per_device(): lax.all_to_all(split_rows(second_pair, blocks), 'mode', split_axis=2, con...  7.31 us
    dot_general x5, matrix products, complex_sums(): jnp.einsum(spec, left_op[0], right_op[1], preferred_element_type=jnp.floa...  6.06 us
    squeeze x1, local copies, waits for them, and re-layouts, per_device(): second_pair = join_pair(leaves[2], leaves[3], join_order[base_index + 1])  5.73 us
    reshape x3, local copies, waits for them, and re-layouts, split_rows(): tensor.reshape(shape[0], shape[1], blocks, shape[2] // blocks, shape[3])  4.91 us
    all_to_all x1, starting transfers between devices, per_device(): lax.all_to_all(split_rows(first_pair, blocks), 'mode', split_axis=2, conc...  4.35 us
  transfers between devices with their start and end apart: 3, of which 3 were waited for; matrix products, arithmetic and copies ran while one was open for 5% of the time, Pallas kernels for 0%

commit v1 on v0

--- a/solution.py
+++ b/solution.py
@@ -2,6 +2,21 @@
 import jax.numpy as jnp
 from jax import lax
 from jax.sharding import PartitionSpec as P
+
+
+def shape_the_forms(target, bus_axis):
+    local_now, seen_now = (lax.axis_size(bus_axis), lax.axis_index(bus_axis))
+    plain = target.shape[2] // local_now
+    frame_out = jnp.roll(target, -seen_now * plain, axis=2)
+    so_far_all = [lax.slice_in_dim(frame_out, 0, plain, axis=2)]
+    for idx in range(1, local_now):
+        top = lax.slice_in_dim(frame_out, idx * plain, (idx + 1) * plain, axis=2)
+        tile_out = lax.ppermute(
+            top, bus_axis, [(dev_i, (dev_i + idx) % local_now) for dev_i in range(local_now)]
+        )
+        so_far_all.append(tile_out)
+    kept_arr = jnp.concatenate(so_far_all[::-1], axis=1)
+    return jnp.roll(kept_arr, shift=(seen_now + 1) * so_far_all[0].shape[1], axis=1)
 
 
 def from_partner(value, axis, bit):
@@ -55,9 +70,7 @@
         lax.all_to_all(
             split_rows(first_pair, blocks), "mode", split_axis=2, concat_axis=1, tiled=True
         ),
-        lax.all_to_all(
-            split_rows(second_pair, blocks), "mode", split_axis=2, concat_axis=1, tiled=True
-        ),
+        shape_the_forms(split_rows(second_pair, blocks), "mode"),
     )
     first_pair = merge_rows(first_pair)
     second_pair = merge_rows(second_pair)

time: 196 us -> 187 us (0.954)
  waiting for transfers between devices: 88.9 us -> 44.5 us
  starting transfers between devices: 11.7 us -> 47.9 us
    all_to_all x1, waiting for transfers between devices: 45.3 us -> 0.01 us  [per_device(): lax.all_to_all(split_rows(first_pair, blocks), 'mode', split_axis=2, conc...]
    ppermute x0 -> x7, waiting for transfers between devices: none -> 42.7 us  [shape_the_forms(): lax.ppermute(top, bus_axis, [(dev_i, (dev_i + idx) % local_now) for dev_i...]
    all_to_all x1 -> x0, waiting for transfers between devices: 41.7 us -> none  [per_device(): lax.all_to_all(split_rows(second_pair, blocks), 'mode', split_axis=2, con...]
    ppermute x0 -> x7, starting transfers between devices: none -> 40.5 us  [shape_the_forms(): lax.ppermute(top, bus_axis, [(dev_i, (dev_i + idx) % local_now) for dev_i...]
    all_to_all x1 -> x0, starting transfers between devices: 7.31 us -> none  [per_device(): lax.all_to_all(split_rows(second_pair, blocks), 'mode', split_axis=2, con...]
    all_to_all x1, starting transfers between devices: 4.35 us -> 7.31 us  [per_device(): lax.all_to_all(split_rows(first_pair, blocks), 'mode', split_axis=2, conc...]
    unnamed x4 -> x22, local copies, waits for them, and re-layouts: 0.01 us -> 2.88 us
    concatenate x0 -> x1, other arithmetic: none -> 2.34 us  [shape_the_forms(): frame_out = jnp.roll(target, -seen_now * plain, axis=2)]
  transfers between devices with their start and end apart: 3 -> 9, of which waited for: 3 -> 5; matrix products, arithmetic and copies ran while one was open for 5% -> 6% of each run, Pallas kernels for 0% -> 0%
where the time goes in v1:
time: 187 us; the launch traced here: 186 us
  blocking collectives  50.3 us (27%)
  starting transfers between devices  47.9 us (26%)
  waiting for transfers between devices  44.5 us (24%)
  local copies, waits for them, and re-layouts  17 us (9%)
  matrix products  15.1 us (8%)
  other arithmetic  8.33 us (4%)
  between operations  2.79 us (1%)
    all_to_all x1, blocking collectives, per_device(): lax.all_to_all(split_rows(middle, blocks), 'mode', split_axis=2, concat_a...  50.3 us
    ppermute x7, waiting for transfers between devices, shape_the_forms(): lax.ppermute(top, bus_axis, [(dev_i, (dev_i + idx) % local_now) for dev_i...  42.7 us
    ppermute x7, starting transfers between devices, shape_the_forms(): lax.ppermute(top, bus_axis, [(dev_i, (dev_i + idx) % local_now) for dev_i...  40.5 us
    all_to_all x1, starting transfers between devices, per_device(): lax.all_to_all(split_rows(first_pair, blocks), 'mode', split_axis=2, conc...  7.31 us
    dot_general x5, matrix products, complex_sums(): jnp.einsum(spec, left_op[0], right_op[1], preferred_element_type=jnp.floa...  6.06 us
    squeeze x1, local copies, waits for them, and re-layouts, per_device(): second_pair = join_pair(leaves[2], leaves[3], join_order[base_index + 1])  5.7 us
  transfers between devices with their start and end apart: 9, of which 5 were waited for; matrix products, arithmetic and copies ran while one was open for 6% of the time, Pallas kernels for 0%

profile of v1, /device:TPU:0, one launch (start us, length us, event | category | flops | bytes accessed | tf_op | source)
XLA Modules:
  0.0 186.2 jit_solution(7001037594515468208)
XLA Ops:
  0.0 5.7 %slice_bitcast_fusion = (bf16[2,2,512,512]{3,2,1,0:T(8,128)(2,1)S(1)}, bf16[2,2,512,512]{3,2,1,0:T(8,128)(2,1)}, bf16[2,2,512,512]{3,2,1,0:T(8,128)(2,1)}, bf16[2,2,512,512]{3,2,1,0:T(8,128)(2,1)}) fusion(bf16[4,2,2,512,512]{4,3,2,1,0:T(8,128)(2,1)} %param.10), kind=kLoop, calls=%fused_computation.130 | loop fusion | bytes 16777216 | tf_op jit(solution)/shard_map/squeeze | solution.py:68
  5.7 0.7 fusion.119
  7.0 6.6 %conditional.6 = (bf16[2,2,512,512]{3,2,1,0:T(8,128)(2,1)}) conditional(s32[]{:T(128)} %bitcast.38, (bf16[2,2,512,512]{3,2,1,0:T(8,128)(2,1)}, bf16[2,2,512,512]{3,2,1,0:T(8,128)(2,1)}) %tuple.32, (bf16[2,2,512,512]{3,2,1,0:T(8,128)(2,1)}, bf16[2,2,512,512]{3,2,1,0:T(8,128)(2,1)}) %tuple.33), branch_computations={%region_0.0_spmd, %region_1.0_spmd} | conditional | flops 2150629376 | bytes 39845952
  7.0 2.4 %fusion.18 = f32[2,512,512]{2,1,0:T(8,128)S(1)} fusion(bf16[2,2,512,512]{3,2,1,0:T(8,128)(2,1)} %get-tuple-element.47, bf16[2,2,512,512]{3,2,1,0:T(8,128)(2,1)} %get-tuple-element.46), kind=kOutput, calls=%fused_computation.24 | convolution fusion | flops 536870912 | bytes 4194304 | tf_op jit(solution)/shard_map/cond/branch_1_fun/bij,bjk->bik/dot_general | solution.py:33
  9.5 0.4 copy-done.5
  9.9 0.7 add_bitcast_fusion.1
  10.6 0.7 fusion.24
  11.3 0.7 subtract_bitcast_fusion.1
  12.0 1.6 pad_maximum_fusion.1
  13.6 3.1 %copy.12 = bf16[2,2,8,64,512]{4,3,1,0,2:T(8,128)(2,1)} copy(bf16[2,2,8,64,512]{4,3,2,1,0:T(8,128)(2,1)} %bitcast.229) | data formatting | bytes 4194304 | tf_op jit(solution)/shard_map/reshape | solution.py:53
  16.7 7.3 %all-to-all-start = ((bf16[2,2,8,64,512]{4,3,1,0,2:T(8,128)(2,1)}), bf16[2,2,8,64,512]{4,3,1,0,2:T(8,128)(2,1)}, u32[]{:S(2)}, u32[]{:S(2)}) async-start(bf16[2,2,8,64,512]{4,3,1,0,2:T(8,128)(2,1)} %copy.12), calls=%async_computation | async-start | bytes 4194304 | tf_op jit(solution)/shard_map/all_to_all | solution.py:70
  24.7 4.5 %conditional.7 = (bf16[2,2,512,512]{3,2,1,0:T(8,128)(2,1)S(1)}) conditional(s32[]{:T(128)} %bitcast.45, (bf16[2,2,512,512]{3,2,1,0:T(8,128)(2,1)}, bf16[2,2,512,512]{3,2,1,0:T(8,128)(2,1)S(1)}) %tuple.34, (bf16[2,2,512,512]{3,2,1,0:T(8,128)(2,1)S(1)}, bf16[2,2,512,512]{3,2,1,0:T(8,128)(2,1)}) %tuple.35), branch_computations={%region_2.0_spmd, %region_3.0_spmd} | conditional | flops 2150629376 | bytes 31457316
  24.7 2.1 %fusion.36 = f32[2,512,512]{2,1,0:T(8,128)S(1)} fusion(bf16[2,2,512,512]{3,2,1,0:T(8,128)(2,1)S(1)} %get-tuple-element.49, bf16[2,2,512,512]{3,2,1,0:T(8,128)(2,1)} %get-tuple-element.48), kind=kOutput, calls=%fused_computation.45 | convolution fusion | flops 536870912 | bytes 4194304 | tf_op jit(solution)/shard_map/cond/branch_0_fun/bij,bjk->bik/dot_general | solution.py:33
  26.8 0.7 add_bitcast_fusion.2
  27.5 0.7 fusion.42
  28.2 0.7 subtract_bitcast_fusion.2
  29.1 1.3 copy-done.6
  30.4 2.3 %fusion.108 = bf16[2,2,8,64,512]{4,3,2,1,0:T(8,128)(2,1)S(1)} fusion(s32[]{:T(128)S(6)} %select_n.67, bf16[2,2,8,64,512]{4,3,2,1,0:T(8,128)(2,1)} %bitcast.230), kind=kLoop, calls=%fused_computation.128 | loop fusion | flops 1048576 | bytes 4194308 | tf_op jit(solution)/shard_map/jit(_roll_dynamic)/concatenate | solution.py:10
  32.8 1.3 slice_bitcast_fusion.25
  34.1 4.7 %collective-permute-start = (bf16[2,2,1,64,512]{4,3,1,0,2:T(8,128)(2,1)}, bf16[2,2,1,64,512]{4,3,1,0,2:T(8,128)(2,1)S(1)}, u32[]{:S(2)}, u32[]{:S(2)}) collective-permute-start(bf16[2,2,1,64,512]{4,3,1,0,2:T(8,128)(2,1)} %get-tuple-element.71), channel_id=1, source_target_pairs={{0,14},{2,0},{4,2},{6,4},{8,6},{10,8},{12,10},{14,12},{1,15},{3,1}... | collective-permute-start | bytes 786440 | tf_op jit(solution)/shard_map/ppermute | solution.py:14
  38.8 0.5 collective-permute-start.1
  39.3 2.9 %collective-permute-start.3 = (bf16[2,2,1,64,512]{4,3,1,0,2:T(8,128)(2,1)}, bf16[2,2,1,64,512]{4,3,1,0,2:T(8,128)(2,1)S(1)}, u32[]{:S(2)}, u32[]{:S(2)}) collective-permute-start(bf16[2,2,1,64,512]{4,3,1,0,2:T(8,128)(2,1)} %get-tuple-element.68), channel_id=1, source_target_pairs={{0,8},{2,10},{4,12},{6,14},{8,0},{10,2},{12,4},{14,6},{1,9},{3,11}... | collective-permute-start | bytes 786440 | tf_op jit(solution)/shard_map/ppermute | solution.py:14
  42.9 23.0 %collective-permute-done = bf16[2,2,1,64,512]{4,3,1,0,2:T(8,128)(2,1)S(1)} collective-permute-done((bf16[2,2,1,64,512]{4,3,1,0,2:T(8,128)(2,1)}, bf16[2,2,1,64,512]{4,3,1,0,2:T(8,128)(2,1)S(1)}, u32[]{:S(2)}, u32[]{:S(2)}) %collective-permute-start) | collective-permute-done | bytes 262176 | tf_op jit(solution)/shard_map/ppermute | solution.py:14
  65.9 5.6 %collective-permute-done.1 = bf16[2,2,1,64,512]{4,3,1,0,2:T(8,128)(2,1)S(1)} collective-permute-done((bf16[2,2,1,64,512]{4,3,1,0,2:T(8,128)(2,1)}, bf16[2,2,1,64,512]{4,3,1,0,2:T(8,128)(2,1)S(1)}, u32[]{:S(2)}, u32[]{:S(2)}) %collective-permute-start.1) | collective-permute-done | bytes 262176 | tf_op jit(solution)/shard_map/ppermute | solution.py:14
  71.5 32.3 %collective-permute-start.6 = (bf16[2,2,1,64,512]{4,3,1,0,2:T(8,128)(2,1)}, bf16[2,2,1,64,512]{4,3,1,0,2:T(8,128)(2,1)S(1)}, u32[]{:S(2)}, u32[]{:S(2)}) collective-permute-start(bf16[2,2,1,64,512]{4,3,1,0,2:T(8,128)(2,1)} %get-tuple-element.65), channel_id=1, source_target_pairs={{0,2},{2,4},{4,6},{6,8},{8,10},{10,12},{12,14},{14,0},{1,3},{3,5},... | collective-permute-start | bytes 786440 | tf_op jit(solution)/shard_map/ppermute | solution.py:14
  103.9 13.3 %collective-permute-done.3 = bf16[2,2,1,64,512]{4,3,1,0,2:T(8,128)(2,1)S(1)} collective-permute-done((bf16[2,2,1,64,512]{4,3,1,0,2:T(8,128)(2,1)}, bf16[2,2,1,64,512]{4,3,1,0,2:T(8,128)(2,1)S(1)}, u32[]{:S(2)}, u32[]{:S(2)}) %collective-permute-start.3) | collective-permute-done | bytes 262176 | tf_op jit(solution)/shard_map/ppermute | solution.py:14
  117.3 0.8 collective-permute-done.4
  118.7 1.8 copy.13
  120.5 3.3 %conditional.8 = (bf16[2,2,512,512]{3,2,1,0:T(8,128)(2,1)S(1)}) conditional(s32[]{:T(128)} %bitcast.37, (bf16[2,2,512,512]{3,2,1,0:T(8,128)(2,1)S(1)}, bf16[2,2,512,512]{3,2,1,0:T(8,128)(2,1)S(1)}) %tuple.61, (bf16[2,2,512,512]{3,2,1,0:T(8,128)(2,1)S(1)}, bf16[2,2,512,512]{3,2,1,0:T(8,128)(2,1)S(1)}) %tuple.62), branch_computations={%region_4.5_spmd, %region_5.6_spmd} | conditional | flops 2150629376 | bytes 23068680
  120.7 0.7 fusion.72
  121.4 0.7 add_bitcast_fusion.4
  122.1 0.7 fusion.78
  122.8 0.7 subtract_bitcast_fusion.4
  124.0 50.3 %all_to_all.30 = bf16[2,2,8,64,512]{4,3,1,0,2:T(8,128)(2,1)S(1)} all-to-all(bf16[2,2,8,64,512]{4,3,1,0,2:T(8,128)(2,1)S(1)} %copy.16), channel_id=1, replica_groups=mesh['cuts'=2,'mode'=8,'branch'=2] {'mode'}, dimensions={2} | all-to-all | bytes 4194304 | tf_op jit(solution)/shard_map/all_to_all | solution.py:79
  175.2 1.7 slice_bitcast_fusion.9
  176.9 0.3 broadcast_select_fusion
  177.1 1.7 collective-permute-done.7
  178.9 2.0 %broadcast_select_fusion.3 = (bf16[2,2,512,512]{3,2,1,0:T(8,128)(2,1)S(1)}, bf16[2,2,512,512]{3,2,1,0:T(8,128)(2,1)S(1)}, bf16[2,2,512,512]{3,2,1,0:T(8,128)(2,1)S(1)}) fusion(pred[]{:T(512)} %bitcast.36, bf16[2,2,512,512]{3,2,1,0:T(8,128)(2,1)} %collective-permute-done.7, bf16[2,2,512,512]{3,2,1,0:T(8,128)(2,1)S(1)} %bitcast.234, pred[]{:T(512)S(6)} %eq.33), kind=kLoop, calls=%fused_computation.137 | loop fusion | flops 3145728 | bytes 10485762 | tf_op jit(solution)/shard_map/jit(_where)/select_n | solution.py:92
  180.9 0.3 dynamic-slice_select_fusion
  181.2 0.4 fusion.114
  181.6 0.4 fusion.113
  182.1 0.4 fusion.111
  182.5 0.4 fusion.116
  183.0 0.4 fusion.115
  183.4 0.4 fusion.112
  183.9 0.4 fusion.109
  184.3 0.4 fusion.110
  184.7 1.5 pad_maximum_fusion.6
  (40 shorter events, 1.5 us)
Async XLA Ops:
  0.0 5.7 %copy-start.7 = (s32[7]{0:T(128)S(1)}, s32[7]{0:T(128)}, u32[]{:S(2)}) copy-start(s32[7]{0:T(128)} %param.11) | copy-start | bytes 88
  7.0 2.4 %copy-start.3 = (bf16[2,2,512,512]{3,2,1,0:T(8,128)(2,1)S(1)}, bf16[2,2,512,512]{3,2,1,0:T(8,128)(2,1)}, u32[]{:S(2)}) copy-start(bf16[2,2,512,512]{3,2,1,0:T(8,128)(2,1)} %get-tuple-element.46) | copy-start | bytes 6291460 | tf_op jit(solution)/shard_map/conditional
  7.0 2.8 %copy-start.5 = (bf16[2,2,512,512]{3,2,1,0:T(8,128)(2,1)S(1)}, bf16[2,2,512,512]{3,2,1,0:T(8,128)(2,1)}, u32[]{:S(2)}) copy-start(bf16[2,2,512,512]{3,2,1,0:T(8,128)(2,1)} %get-tuple-element.47) | copy-start | bytes 6291460 | tf_op jit(solution)/shard_map/conditional
  16.7 102.0 %all-to-all-start = ((bf16[2,2,8,64,512]{4,3,1,0,2:T(8,128)(2,1)}), bf16[2,2,8,64,512]{4,3,1,0,2:T(8,128)(2,1)}, u32[]{:S(2)}, u32[]{:S(2)}) async-start(bf16[2,2,8,64,512]{4,3,1,0,2:T(8,128)(2,1)} %copy.12), calls=%async_computation | async-start | bytes 4194304 | tf_op jit(solution)/shard_map/all_to_all | solution.py:70
  24.7 2.1 %copy-start = (bf16[2,2,512,512]{3,2,1,0:T(8,128)(2,1)S(1)}, bf16[2,2,512,512]{3,2,1,0:T(8,128)(2,1)}, u32[]{:S(2)}) copy-start(bf16[2,2,512,512]{3,2,1,0:T(8,128)(2,1)} %get-tuple-element.48) | copy-start | bytes 6291460 | tf_op jit(solution)/shard_map/conditional.1
  29.1 1.3 copy-start.6
  34.1 31.8 %collective-permute-start = (bf16[2,2,1,64,512]{4,3,1,0,2:T(8,128)(2,1)}, bf16[2,2,1,64,512]{4,3,1,0,2:T(8,128)(2,1)S(1)}, u32[]{:S(2)}, u32[]{:S(2)}) collective-permute-start(bf16[2,2,1,64,512]{4,3,1,0,2:T(8,128)(2,1)} %get-tuple-element.71), channel_id=1, source_target_pairs={{0,14},{2,0},{4,2},{6,4},{8,6},{10,8},{12,10},{14,12},{1,15},{3,1}... | collective-permute-start | bytes 786440 | tf_op jit(solution)/shard_map/ppermute | solution.py:14
  38.8 32.7 %collective-permute-start.1 = (bf16[2,2,1,64,512]{4,3,1,0,2:T(8,128)(2,1)}, bf16[2,2,1,64,512]{4,3,1,0,2:T(8,128)(2,1)S(1)}, u32[]{:S(2)}, u32[]{:S(2)}) collective-permute-start(bf16[2,2,1,64,512]{4,3,1,0,2:T(8,128)(2,1)} %get-tuple-element.70), channel_id=1, source_target_pairs={{0,12},{2,14},{4,0},{6,2},{8,4},{10,6},{12,8},{14,10},{1,13},{3,15... | collective-permute-start | bytes 786440 | tf_op jit(solution)/shard_map/ppermute | solution.py:14
  39.3 64.5 %collective-permute-start.2 = (bf16[2,2,1,64,512]{4,3,1,0,2:T(8,128)(2,1)}, bf16[2,2,1,64,512]{4,3,1,0,2:T(8,128)(2,1)S(1)}, u32[]{:S(2)}, u32[]{:S(2)}) collective-permute-start(bf16[2,2,1,64,512]{4,3,1,0,2:T(8,128)(2,1)} %get-tuple-element.69), channel_id=1, source_target_pairs={{0,10},{2,12},{4,14},{6,0},{8,2},{10,4},{12,6},{14,8},{1,11},{3,13... | collective-permute-start | bytes 786440 | tf_op jit(solution)/shard_map/ppermute | solution.py:14
  39.3 77.9 %collective-permute-start.3 = (bf16[2,2,1,64,512]{4,3,1,0,2:T(8,128)(2,1)}, bf16[2,2,1,64,512]{4,3,1,0,2:T(8,128)(2,1)S(1)}, u32[]{:S(2)}, u32[]{:S(2)}) collective-permute-start(bf16[2,2,1,64,512]{4,3,1,0,2:T(8,128)(2,1)} %get-tuple-element.68), channel_id=1, source_target_pairs={{0,8},{2,10},{4,12},{6,14},{8,0},{10,2},{12,4},{14,6},{1,9},{3,11}... | collective-permute-start | bytes 786440 | tf_op jit(solution)/shard_map/ppermute | solution.py:14
  42.3 75.8 %collective-permute-start.4 = (bf16[2,2,1,64,512]{4,3,1,0,2:T(8,128)(2,1)}, bf16[2,2,1,64,512]{4,3,1,0,2:T(8,128)(2,1)S(1)}, u32[]{:S(2)}, u32[]{:S(2)}) collective-permute-start(bf16[2,2,1,64,512]{4,3,1,0,2:T(8,128)(2,1)} %get-tuple-element.67), channel_id=1, source_target_pairs={{0,6},{2,8},{4,10},{6,12},{8,14},{10,0},{12,2},{14,4},{1,7},{3,9},... | collective-permute-start | bytes 786440 | tf_op jit(solution)/shard_map/ppermute | solution.py:14
  65.9 52.2 %collective-permute-start.5 = (bf16[2,2,1,64,512]{4,3,1,0,2:T(8,128)(2,1)}, bf16[2,2,1,64,512]{4,3,1,0,2:T(8,128)(2,1)S(1)}, u32[]{:S(2)}, u32[]{:S(2)}) collective-permute-start(bf16[2,2,1,64,512]{4,3,1,0,2:T(8,128)(2,1)} %get-tuple-element.66), channel_id=1, source_target_pairs={{0,4},{2,6},{4,8},{6,10},{8,12},{10,14},{12,0},{14,2},{1,5},{3,7},... | collective-permute-start | bytes 786440 | tf_op jit(solution)/shard_map/ppermute | solution.py:14
  71.5 46.7 %collective-permute-start.6 = (bf16[2,2,1,64,512]{4,3,1,0,2:T(8,128)(2,1)}, bf16[2,2,1,64,512]{4,3,1,0,2:T(8,128)(2,1)S(1)}, u32[]{:S(2)}, u32[]{:S(2)}) collective-permute-start(bf16[2,2,1,64,512]{4,3,1,0,2:T(8,128)(2,1)} %get-tuple-element.65), channel_id=1, source_target_pairs={{0,2},{2,4},{4,6},{6,8},{8,10},{10,12},{12,14},{14,0},{1,3},{3,5},... | collective-permute-start | bytes 786440 | tf_op jit(solution)/shard_map/ppermute | solution.py:14
  174.3 0.9 copy-start.8
  174.5 4.4 %collective-permute-start.7 = (bf16[2,2,512,512]{3,2,1,0:T(8,128)(2,1)S(1)}, bf16[2,2,512,512]{3,2,1,0:T(8,128)(2,1)}, u32[]{:S(2)}, u32[]{:S(2)}) collective-permute-start(bf16[2,2,512,512]{3,2,1,0:T(8,128)(2,1)S(1)} %bitcast.233), channel_id=1, source_target_pairs={{0,1},{1,0},{2,3},{3,2},{4,5},{5,4},{6,7},{7,6},{8,9},{9,8},{10,11... | collective-permute-start | bytes 6291464 | tf_op jit(solution)/shard_map/ppermute | solution.py:25
